TPU v7x, 32 devices: a whole 2x2x4 slice. The times are simulated.
32 devices in a mesh: groups: 2 (over y), row: 8 (over z, x), col: 2 (over core).
Axes of the slice: x: 2, y: 2, z: 4, core: 2. Of those that a mesh axis runs over, the one named last changes fastest.
Arguments:
- wavenumber: float32 [2], P('groups'), parts along dimension 0, may hold values from 30 to 90
- tgt_geom: float32 [6, 4096], P(None, ('groups', 'row')), parts along dimension 1, may hold values from -2 to 8, as said below
- src_geom: float32 [4, 512], P(None, ('groups', 'row', 'col')), parts along dimension 1, may hold values from -2 to 8, as said below
- excite: bfloat16 [128, 512], P(None, ('groups', 'row', 'col')), parts along dimension 1, may hold values from -6 to 6
- tgt_nodes: float32 [3, 6144], P(None, ('groups', 'row')), parts along dimension 1, may hold values from -2 to 8, as said below
- src_nodes: float32 [3, 3072], P(None, ('groups', 'row')), parts along dimension 1, may hold values from -2 to 8, as said below
- tgt_weights: bfloat16 [2, 192, 4096], P(None, None, ('groups', 'row')), parts along dimension 2, may hold values from -0.109375 to 0.109375
- src_weights: bfloat16 [2, 192, 512], P(None, None, ('groups', 'row', 'col')), parts along dimension 2, may hold values from -1 to 1
- near_order: int32 [32, 9], P(('groups', 'row')), parts along dimension 0, may hold values from 0 to 3
Outputs:
- responses: float32 [4096, 128], P(('groups', 'row', 'col')), parts along dimension 0
There are 2 independent parts, one for each index of `groups`. A program takes and returns all parts, laid end to end along the dimension named above; each array names one. Nothing has to cross between parts.
Inputs may be any that keep to these rules, and one draw needn't show every extreme that they name: `tgt_geom`: rows 0 to 2 are points, rows 3 to 5 unit normals. `src_geom`: rows 0 to 2 are points, row 3 positive areas. `tgt_nodes`: Points. `src_nodes`: Points. `near_order`: 0 marks a pair that is not near.
All inputs are finite; a program needn't handle non-finite values.
Results may differ from a plain program's by a relative error of at most 0.0011.
Values may be sent and summed in bfloat16 or wider, within the bound.
A program may use at most 64 MiB of HBM per device.

v0:
```python
import functools
import math

import jax
import jax.numpy as jnp
import numpy as np
from jax import lax
from jax.experimental import pallas as pl
from jax.experimental.pallas import tpu as pltpu
from jax.sharding import PartitionSpec as P

ORDERS = 3
SOFT = 0.05
FOUR_PI = 4.0 * math.pi
LANES = 128
MESH = pl.DeviceIdType.MESH
TN = (((0,), (0,)), ((), ()))


def fitted(function, terms):
    nodes = (np.cos((np.arange(terms) + 0.5) * np.pi / terms) + 1.0) / 8.0
    matrix = np.vander(nodes, terms, increasing=True)
    return [float(c) for c in np.linalg.solve(matrix, function(np.sqrt(nodes)))]


COS = fitted(lambda u: np.cos(2.0 * np.pi * u), 7)
SIN = fitted(lambda u: np.sin(2.0 * np.pi * u) / u, 7)


def horner(coefficients, y):
    total = coefficients[-1]
    for c in coefficients[-2::-1]:
        total = total * y + c
    return total


def cos_sin(turns):
    u = turns - jnp.round(turns)
    y = u * u
    return horner(COS, y), u * horner(SIN, y)


def times_i(value):
    half = value.shape[1] // 2
    swapped = jnp.concatenate([value[:, half:], value[:, :half]], 1)
    lane = lax.broadcasted_iota(jnp.int32, value.shape, 1)
    return jnp.where(lane < half, -swapped, swapped)


def split_two(value):
    high = value.astype(jnp.bfloat16)
    return high, (value - high.astype(jnp.float32)).astype(jnp.bfloat16)


def columns_of(rows):
    few, lanes = rows.shape
    pad = jnp.zeros((8 - few, lanes), jnp.float32)
    return jnp.concatenate([rows, pad], 0).T


def kernel(
    wave_ref,
    order_ref,
    tgt_ref,
    tnode_ref,
    tweight_ref,
    geom_hbm,
    excite_hbm,
    snode_hbm,
    sweight_hbm,
    out_ref,
    node_all,
    weight_all,
    geom_all,
    excite_all,
    green,
    node_send,
    weight_send,
    geom_send,
    excite_send,
    recv,
    pair_send,
    pair_recv,
):
    n_row = lax.axis_size("row")
    row = lax.axis_index("row")
    col = lax.axis_index("col")
    other = 1 - col
    band = node_all.shape[0]
    reach = (band - 1) // 2
    qn = node_all.shape[2]
    qpad = pl.cdiv(qn, LANES) * LANES
    step_nodes = qn // ORDERS
    per = excite_hbm.shape[0]
    blk = out_ref.shape[0]

    barrier = pltpu.get_barrier_semaphore()

    @pl.loop(1, n_row)
    def _(d):
        pl.semaphore_signal(
            barrier, inc=1, device_id={"row": lax.rem(row + d, n_row)}, device_id_type=MESH
        )

    pl.semaphore_signal(barrier, inc=1, device_id={"col": other}, device_id_type=MESH)

    def fill(slot):
        pltpu.make_async_copy(snode_hbm, node_all.at[slot], recv.at[0]).start()
        pltpu.make_async_copy(sweight_hbm, weight_all.at[col, slot], recv.at[1]).start()

    @pl.loop(0, band)
    def _(slot):
        block = row + slot - reach
        missing = jnp.logical_or(block < 0, block >= n_row)

        @pl.when(jnp.logical_or(missing, slot == reach))
        def _():
            fill(slot)

    pltpu.make_async_copy(geom_hbm, geom_all.at[col, row], recv.at[2]).start()
    pltpu.make_async_copy(excite_hbm, excite_all.at[col, row], recv.at[3]).start()

    pl.semaphore_wait(barrier, n_row)

    def near_copies(slot):
        to = {"row": row + reach - slot}
        nodes = pltpu.make_async_remote_copy(
            src_ref=snode_hbm,
            dst_ref=node_all.at[slot],
            send_sem=node_send.at[slot],
            recv_sem=recv.at[0],
            device_id=to,
            device_id_type=MESH,
        )
        weights = pltpu.make_async_remote_copy(
            src_ref=sweight_hbm,
            dst_ref=weight_all.at[col, slot],
            send_sem=weight_send.at[slot],
            recv_sem=recv.at[1],
            device_id=to,
            device_id_type=MESH,
        )
        return nodes, weights

    def far_copies(d):
        to = {"row": lax.rem(row + d, n_row)}
        geoms = pltpu.make_async_remote_copy(
            src_ref=geom_hbm,
            dst_ref=geom_all.at[col, row],
            send_sem=geom_send.at[d],
            recv_sem=recv.at[2],
            device_id=to,
            device_id_type=MESH,
        )
        excites = pltpu.make_async_remote_copy(
            src_ref=excite_hbm,
            dst_ref=excite_all.at[col, row],
            send_sem=excite_send.at[d],
            recv_sem=recv.at[3],
            device_id=to,
            device_id_type=MESH,
        )
        return geoms, excites

    def for_near(act):
        @pl.loop(0, band)
        def _(slot):
            goal = row + reach - slot
            inside = jnp.logical_and(goal >= 0, goal < n_row)

            @pl.when(jnp.logical_and(inside, slot != reach))
            def _():
                act(slot)

    for_near(lambda slot: near_copies(slot)[0].start())

    @pl.loop(1, n_row)
    def _(d):
        far_copies(d)[0].start()

    for_near(lambda slot: near_copies(slot)[1].start())

    @pl.loop(1, n_row)
    def _(d):
        far_copies(d)[1].start()

    def to_pair(index, buffer):
        return pltpu.make_async_remote_copy(
            src_ref=buffer.at[col],
            dst_ref=buffer.at[col],
            send_sem=pair_send.at[index],
            recv_sem=pair_recv.at[index],
            device_id={"col": other},
            device_id_type=MESH,
        )

    def from_pair(index, buffer):
        return pltpu.make_async_remote_copy(
            src_ref=buffer.at[other],
            dst_ref=buffer.at[other],
            send_sem=pair_send.at[index],
            recv_sem=pair_recv.at[index],
            device_id={"col": other},
            device_id_type=MESH,
        )

    wave = wave_ref[0]
    per_turn = wave * (0.5 / math.pi)

    tnodes = tnode_ref[...]
    tnodes = jnp.where(col == 0, tnodes[:, :qn], tnodes[:, qn:])
    if qpad > qn:
        tnodes = jnp.concatenate([tnodes, jnp.zeros((3, qpad - qn), jnp.float32)], 1)
    tcols = columns_of(tnodes)[:qn]
    t_x, t_y, t_z = (jnp.broadcast_to(tcols[:, i : i + 1], (qn, LANES)) for i in range(3))

    pltpu.make_async_copy(node_all, node_all, recv.at[0]).wait()

    @pl.loop(0, band)
    def _(slot):
        snodes = node_all[slot]
        if qpad > qn:
            snodes = jnp.concatenate([snodes, jnp.zeros((3, qpad - qn), jnp.float32)], 1)
        for part in range(qpad // LANES):
            here = slice(part * LANES, (part + 1) * LANES)
            d_x = t_x - snodes[0:1, here]
            d_y = t_y - snodes[1:2, here]
            d_z = t_z - snodes[2:3, here]
            squared = d_x * d_x + d_y * d_y + d_z * d_z + SOFT * SOFT
            inverse = lax.rsqrt(squared)
            cosine, sine = cos_sin(per_turn * (squared * inverse))
            for index, value in enumerate((inverse * cosine, inverse * sine)):
                high, low = split_two(value)
                at = index * qpad + part * LANES
                green[slot, 0, :, at : at + LANES] = high
                green[slot, 1, :, at : at + LANES] = low

    pltpu.make_async_copy(geom_all.at[col], geom_all.at[col], recv.at[2]).wait()
    to_pair(0, geom_all).start()
    pltpu.make_async_copy(weight_all.at[col], weight_all.at[col], recv.at[1]).wait()
    to_pair(1, weight_all).start()
    pltpu.make_async_copy(excite_all.at[col], excite_all.at[col], recv.at[3]).wait()
    to_pair(2, excite_all).start()
    from_pair(0, geom_all).wait_recv()

    begin = pl.multiple_of(col * blk, blk)
    gcols = columns_of(tgt_ref[:, pl.ds(begin, blk)])
    p_x, p_y, p_z, n_x, n_y, n_z = (gcols[:, i : i + 1] for i in range(6))
    pieces = LANES // per
    chunks = n_row // pieces

    def impedance(half, chunk):
        places = jnp.concatenate([geom_all[half, chunk * pieces + i] for i in range(pieces)], 1)
        d_x = p_x - places[0:1]
        d_y = p_y - places[1:2]
        d_z = p_z - places[2:3]
        squared = d_x * d_x + d_y * d_y + d_z * d_z + SOFT * SOFT
        inverse = lax.rsqrt(squared)
        radius = squared * inverse
        along = (n_x * d_x + n_y * d_y + n_z * d_z) * inverse
        scale = places[3:4] * (inverse * (1.0 / FOUR_PI))
        cosine, sine = cos_sin(per_turn * radius)
        green_re = scale * cosine
        green_im = scale * sine
        factor_re = 1.0 - along
        factor_im = -along / (wave * radius)
        kern_re = green_re * factor_re - green_im * factor_im
        kern_im = green_re * factor_im + green_im * factor_re
        return jnp.concatenate(
            [kern_re.astype(jnp.bfloat16), kern_im.astype(jnp.bfloat16)], 1
        )

    def both(rows):
        turned = times_i(rows.astype(jnp.float32)).astype(jnp.bfloat16)
        return jnp.concatenate([rows, turned], 0)

    from_pair(2, excite_all).wait_recv()

    def far_step(index, total):
        half, chunk = index // chunks, lax.rem(index, chunks)
        rows = excite_all[half, pl.ds(chunk * pieces, pieces)].reshape(LANES, blk)
        return total + jnp.dot(
            impedance(half, chunk), both(rows), preferred_element_type=jnp.float32
        )

    far = lax.fori_loop(0, 2 * chunks, far_step, jnp.zeros(out_ref.shape, jnp.float32))

    from_pair(1, weight_all).wait_recv()
    width = out_ref.shape[1]
    node_index = lax.broadcasted_iota(jnp.int32, (qpad, width), 0)

    def near_step(slot, total):
        block = row + slot - reach
        valid = jnp.logical_and(block >= 0, block < n_row)
        live = jnp.where(valid, order_ref[col, slot] * step_nodes, 0)
        source = jnp.clip(block, 0, n_row - 1)
        stack = []
        for part in range(2):
            for half in range(2):
                stack.append(weight_all[half, slot, part])
        weights = jnp.concatenate(stack, 0)
        if qpad > qn:
            weights = jnp.concatenate(
                [weights, jnp.zeros((weights.shape[0], qpad - qn), jnp.bfloat16)], 1
            )
        rows = jnp.concatenate([excite_all[half, source] for half in range(2)], 0)
        moments = lax.dot_general(weights, both(rows), TN, preferred_element_type=jnp.float32)
        moments = jnp.where(node_index < live, moments * (1.0 / FOUR_PI), 0.0)
        full = jnp.concatenate([moments, times_i(moments)], 0)
        high, low = split_two(full)
        product = jnp.dot(
            green[slot, 0],
            jnp.concatenate([high, low], 1),
            preferred_element_type=jnp.float32,
        )
        product = (
            product[:, :width]
            + product[:, width:]
            + jnp.dot(green[slot, 1], high, preferred_element_type=jnp.float32)
        )
        return total + jnp.where(node_index[:qn] < live, product, 0.0)

    inner = lax.fori_loop(0, band, near_step, jnp.zeros((qn, width), jnp.float32))
    tests = jnp.concatenate(
        [tweight_ref[0, :, pl.ds(begin, blk)], tweight_ref[1, :, pl.ds(begin, blk)]], 0
    )
    high, low = split_two(jnp.concatenate([inner, times_i(inner)], 0))
    product = lax.dot_general(
        tests, jnp.concatenate([high, low], 1), TN, preferred_element_type=jnp.float32
    )
    out_ref[...] = far + (product[:, :width] + product[:, width:])

    for_near(lambda slot: [copy.wait_send() for copy in near_copies(slot)])

    @pl.loop(1, n_row)
    def _(d):
        for copy in far_copies(d):
            copy.wait_send()

    for index, buffer in enumerate((geom_all, weight_all, excite_all)):
        to_pair(index, buffer).wait_send()


def on_device(
    wavenumber,
    tgt_geom,
    src_geom,
    excite,
    tgt_nodes,
    src_nodes,
    tgt_weights,
    src_weights,
    near_order,
):
    n_row = lax.axis_size("row")
    band = near_order.shape[1]
    blk = tgt_geom.shape[1] // lax.axis_size("col")
    qn = src_nodes.shape[1]
    qpad = -(-qn // LANES) * LANES
    excite_rows = excite.T
    weight_rows = src_weights.transpose(0, 2, 1)
    vmem = pl.BlockSpec(memory_space=pltpu.VMEM)
    smem = pl.BlockSpec(memory_space=pltpu.SMEM)
    hbm = pl.BlockSpec(memory_space=pl.ANY)
    dma = pltpu.SemaphoreType.DMA
    return pl.pallas_call(
        kernel,
        out_shape=jax.ShapeDtypeStruct((blk, excite.shape[0]), jnp.float32),
        in_specs=[smem, smem, vmem, vmem, vmem, hbm, hbm, hbm, hbm],
        out_specs=vmem,
        scratch_shapes=[
            pltpu.VMEM((band,) + src_nodes.shape, jnp.float32),
            pltpu.VMEM((2, band) + weight_rows.shape, jnp.bfloat16),
            pltpu.VMEM((2, n_row) + src_geom.shape, jnp.float32),
            pltpu.VMEM((2, n_row) + excite_rows.shape, jnp.bfloat16),
            pltpu.VMEM((band, 2, qn, 2 * qpad), jnp.bfloat16),
            dma((band,)),
            dma((band,)),
            dma((n_row,)),
            dma((n_row,)),
            dma((4,)),
            dma((3,)),
            dma((3,)),
        ],
        compiler_params=pltpu.CompilerParams(collective_id=0, has_side_effects=True),
        name="slab",
    )(
        wavenumber,
        near_order,
        tgt_geom,
        tgt_nodes,
        tgt_weights,
        src_geom,
        excite_rows,
        src_nodes,
        weight_rows,
    )


def solution(mesh):
    return jax.shard_map(
        on_device,
        mesh=mesh,
        in_specs=(
            P("groups"),
            P(None, ("groups", "row")),
            P(None, ("groups", "row", "col")),
            P(None, ("groups", "row", "col")),
            P(None, ("groups", "row")),
            P(None, ("groups", "row")),
            P(None, None, ("groups", "row")),
            P(None, None, ("groups", "row", "col")),
            P(("groups", "row"), None),
        ),
        out_specs=P(("groups", "row", "col"), None),
        check_vma=False,
    )
```

profile of v0, /device:TPU:1, one launch (start us, length us, event | category | flops | bytes accessed | tf_op | source)
XLA Modules:
  0.0 23.0 jit_solution(5986616784481712747)
XLA Ops:
  0.7 20.9 %slab.1 = f32[128,128]{1,0:T(8,128)} custom-call(f32[1]{0:T(128)S(6)} %copy.11.wave_ref, s32[2,9]{1,0:T(2,128)} %order_ref.1, f32[6,256]{1,0:T(8,128)} %tgt_ref.1, f32[3,384]{1,0:T(4,128)} %tnode_ref.1, bf16[2,192,256]{2,1,0:T(8,128)(2,1)} %tweight_ref.1, f32[4,16]{1,0:T(4,128)} %geom_hbm.1, bf16[16,128]{1,0:T(8,128)(2,1)} %bitcast.3, f32[3,192]{1,0:T(4,128)} %snode_hbm.1, ...), custom_call_target="tpu_custom_call" | custom-call | tf_op jit(solution)/shard_map/slab/pallas_call | solution.py:366
  21.6 1.5 %copy.12 = f32[128,128]{1,0:T(8,128)} copy(f32[128,128]{1,0:T(8,128)} %slab.1) | data formatting | bytes 131072
where the time goes:
time: 23.2 us; the launch traced here: 23 us
  Pallas kernels  20.9 us (90%)
  local copies, waits for them, and re-layouts  1.47 us (6%)
  between operations  0.66 us (3%)
    pallas_call x1, Pallas kernels, on_device(): pl.pallas_call(kernel, out_shape=jax.ShapeDtypeStruct((blk, excite.shape[...  20.9 us
    unnamed x1, local copies, waits for them, and re-layouts  1.47 us

commit v1 on v0

--- a/solution.py
+++ b/solution.py
@@ -15,6 +15,7 @@
 LANES = 128
 MESH = pl.DeviceIdType.MESH
 TN = (((0,), (0,)), ((), ()))
+NT = (((1,), (1,)), ((), ()))
 
 
 def fitted(function, terms):
@@ -59,11 +60,11 @@
 
 
 def kernel(
-    wave_ref,
-    order_ref,
-    tgt_ref,
-    tnode_ref,
-    tweight_ref,
+    wave_hbm,
+    order_hbm,
+    tgt_hbm,
+    tnode_hbm,
+    tweight_hbm,
     geom_hbm,
     excite_hbm,
     snode_hbm,
@@ -73,12 +74,23 @@
     weight_all,
     geom_all,
     excite_all,
-    green,
+    green_high,
+    green_low,
+    wave_ref,
+    order_ref,
+    tgt_ref,
+    tnode_ref,
+    tweight_ref,
+    node_own,
+    local,
     node_send,
     weight_send,
     geom_send,
     excite_send,
     recv,
+    weight_recv,
+    weight_pair,
+    weight_back,
     pair_send,
     pair_recv,
 ):
@@ -104,9 +116,26 @@
 
     pl.semaphore_signal(barrier, inc=1, device_id={"col": other}, device_id_type=MESH)
 
+    loads = [
+        pltpu.make_async_copy(here, there, local.at[index])
+        for index, (here, there) in enumerate(
+            (
+                (wave_hbm, wave_ref),
+                (tnode_hbm, tnode_ref),
+                (order_hbm, order_ref),
+                (tgt_hbm, tgt_ref),
+                (tweight_hbm, tweight_ref),
+            )
+        )
+    ]
+    own_nodes = pltpu.make_async_copy(snode_hbm, node_own, local.at[len(loads)])
+    own_nodes.start()
+    for load in loads:
+        load.start()
+
     def fill(slot):
         pltpu.make_async_copy(snode_hbm, node_all.at[slot], recv.at[0]).start()
-        pltpu.make_async_copy(sweight_hbm, weight_all.at[col, slot], recv.at[1]).start()
+        pltpu.make_async_copy(sweight_hbm, weight_all.at[col, slot], weight_recv.at[slot]).start()
 
     @pl.loop(0, band)
     def _(slot):
@@ -119,8 +148,6 @@
 
     pltpu.make_async_copy(geom_hbm, geom_all.at[col, row], recv.at[2]).start()
     pltpu.make_async_copy(excite_hbm, excite_all.at[col, row], recv.at[3]).start()
-
-    pl.semaphore_wait(barrier, n_row)
 
     def near_copies(slot):
         to = {"row": row + reach - slot}
@@ -136,7 +163,7 @@
             src_ref=sweight_hbm,
             dst_ref=weight_all.at[col, slot],
             send_sem=weight_send.at[slot],
-            recv_sem=recv.at[1],
+            recv_sem=weight_recv.at[slot],
             device_id=to,
             device_id_type=MESH,
         )
@@ -172,17 +199,15 @@
             def _():
                 act(slot)
 
-    for_near(lambda slot: near_copies(slot)[0].start())
-
-    @pl.loop(1, n_row)
-    def _(d):
-        far_copies(d)[0].start()
-
-    for_near(lambda slot: near_copies(slot)[1].start())
-
-    @pl.loop(1, n_row)
-    def _(d):
-        far_copies(d)[1].start()
+    def weight_to_pair(slot, half):
+        return pltpu.make_async_remote_copy(
+            src_ref=weight_all.at[half, slot],
+            dst_ref=weight_all.at[half, slot],
+            send_sem=weight_pair.at[slot],
+            recv_sem=weight_back.at[slot],
+            device_id={"col": other},
+            device_id_type=MESH,
+        )
 
     def to_pair(index, buffer):
         return pltpu.make_async_remote_copy(
@@ -204,6 +229,8 @@
             device_id_type=MESH,
         )
 
+    for load in loads[:3]:
+        load.wait()
     wave = wave_ref[0]
     per_turn = wave * (0.5 / math.pi)
 
@@ -214,11 +241,15 @@
     tcols = columns_of(tnodes)[:qn]
     t_x, t_y, t_z = (jnp.broadcast_to(tcols[:, i : i + 1], (qn, LANES)) for i in range(3))
 
-    pltpu.make_async_copy(node_all, node_all, recv.at[0]).wait()
-
-    @pl.loop(0, band)
-    def _(slot):
-        snodes = node_all[slot]
+    point = lax.broadcasted_iota(jnp.int32, (qn, LANES), 0)
+
+    def order_of(slot):
+        block = row + slot - reach
+        valid = jnp.logical_and(block >= 0, block < n_row)
+        return jnp.where(valid, order_ref[col, slot] * step_nodes, 0)
+
+    def green_of(slot, snodes):
+        live = point < order_of(slot)
         if qpad > qn:
             snodes = jnp.concatenate([snodes, jnp.zeros((3, qpad - qn), jnp.float32)], 1)
         for part in range(qpad // LANES):
@@ -229,20 +260,65 @@
             squared = d_x * d_x + d_y * d_y + d_z * d_z + SOFT * SOFT
             inverse = lax.rsqrt(squared)
             cosine, sine = cos_sin(per_turn * (squared * inverse))
+            inverse = jnp.where(live, inverse, 0.0)
             for index, value in enumerate((inverse * cosine, inverse * sine)):
                 high, low = split_two(value)
-                at = index * qpad + part * LANES
-                green[slot, 0, :, at : at + LANES] = high
-                green[slot, 1, :, at : at + LANES] = low
-
+                at = pl.multiple_of((2 * slot + index) * qpad + part * LANES, LANES)
+                green_high[:, pl.ds(at, LANES)] = high
+                green_low[:, pl.ds(at, LANES)] = low
+
+    own_nodes.wait()
+    green_of(reach, node_own[...])
+
+    pl.semaphore_wait(barrier, n_row)
+
+    for_near(lambda slot: near_copies(slot)[0].start())
+
+    @pl.loop(1, n_row)
+    def _(d):
+        far_copies(d)[0].start()
+
+    for_near(lambda slot: near_copies(slot)[1].start())
+
+    @pl.loop(1, n_row)
+    def _(d):
+        far_copies(d)[1].start()
+
+    pltpu.make_async_copy(node_all, node_all, recv.at[0]).wait()
+
+    def green_some(begin, end):
+        @pl.loop(begin, end)
+        def _(slot):
+            block = row + slot - reach
+            needed = jnp.logical_and(block >= 0, block < n_row)
+
+            @pl.when(jnp.logical_and(needed, slot != reach))
+            def _():
+                green_of(slot, node_all[slot])
+
+            @pl.when(jnp.logical_not(needed))
+            def _():
+                at = pl.ds(pl.multiple_of(2 * slot * qpad, LANES), 2 * qpad)
+                green_high[:, at] = jnp.zeros((qn, 2 * qpad), jnp.bfloat16)
+                green_low[:, at] = jnp.zeros((qn, 2 * qpad), jnp.bfloat16)
+
+    green_some(0, (band - 2))
     pltpu.make_async_copy(geom_all.at[col], geom_all.at[col], recv.at[2]).wait()
     to_pair(0, geom_all).start()
-    pltpu.make_async_copy(weight_all.at[col], weight_all.at[col], recv.at[1]).wait()
-    to_pair(1, weight_all).start()
+
+    @pl.loop(0, band)
+    def _(slot):
+        pltpu.make_async_copy(
+            weight_all.at[col, slot], weight_all.at[col, slot], weight_recv.at[slot]
+        ).wait()
+        weight_to_pair(slot, col).start()
+
     pltpu.make_async_copy(excite_all.at[col], excite_all.at[col], recv.at[3]).wait()
-    to_pair(2, excite_all).start()
+    to_pair(1, excite_all).start()
+    green_some((band - 2), band)
     from_pair(0, geom_all).wait_recv()
 
+    loads[3].wait()
     begin = pl.multiple_of(col * blk, blk)
     gcols = columns_of(tgt_ref[:, pl.ds(begin, blk)])
     p_x, p_y, p_z, n_x, n_y, n_z = (gcols[:, i : i + 1] for i in range(6))
@@ -274,7 +350,7 @@
         turned = times_i(rows.astype(jnp.float32)).astype(jnp.bfloat16)
         return jnp.concatenate([rows, turned], 0)
 
-    from_pair(2, excite_all).wait_recv()
+    from_pair(1, excite_all).wait_recv()
 
     def far_step(index, total):
         half, chunk = index // chunks, lax.rem(index, chunks)
@@ -285,42 +361,42 @@
 
     far = lax.fori_loop(0, 2 * chunks, far_step, jnp.zeros(out_ref.shape, jnp.float32))
 
-    from_pair(1, weight_all).wait_recv()
     width = out_ref.shape[1]
-    node_index = lax.broadcasted_iota(jnp.int32, (qpad, width), 0)
-
-    def near_step(slot, total):
-        block = row + slot - reach
-        valid = jnp.logical_and(block >= 0, block < n_row)
-        live = jnp.where(valid, order_ref[col, slot] * step_nodes, 0)
-        source = jnp.clip(block, 0, n_row - 1)
-        stack = []
+
+    lane = lax.broadcasted_iota(jnp.int32, (2 * per, qpad), 1)
+    applied, sources = [], []
+    for slot in range(band):
+        weight_to_pair(slot, other).wait_recv()
+        live = lane < order_of(slot)
+        basis = []
         for part in range(2):
-            for half in range(2):
-                stack.append(weight_all[half, slot, part])
-        weights = jnp.concatenate(stack, 0)
-        if qpad > qn:
-            weights = jnp.concatenate(
-                [weights, jnp.zeros((weights.shape[0], qpad - qn), jnp.bfloat16)], 1
-            )
-        rows = jnp.concatenate([excite_all[half, source] for half in range(2)], 0)
-        moments = lax.dot_general(weights, both(rows), TN, preferred_element_type=jnp.float32)
-        moments = jnp.where(node_index < live, moments * (1.0 / FOUR_PI), 0.0)
-        full = jnp.concatenate([moments, times_i(moments)], 0)
-        high, low = split_two(full)
-        product = jnp.dot(
-            green[slot, 0],
-            jnp.concatenate([high, low], 1),
-            preferred_element_type=jnp.float32,
-        )
-        product = (
-            product[:, :width]
-            + product[:, width:]
-            + jnp.dot(green[slot, 1], high, preferred_element_type=jnp.float32)
-        )
-        return total + jnp.where(node_index[:qn] < live, product, 0.0)
-
-    inner = lax.fori_loop(0, band, near_step, jnp.zeros((qn, width), jnp.float32))
+            value = jnp.concatenate([weight_all[half, slot, part] for half in range(2)], 0)
+            if qpad > qn:
+                value = jnp.concatenate(
+                    [value, jnp.zeros((2 * per, qpad - qn), jnp.bfloat16)], 1
+                )
+            basis.append(jnp.where(live, value.astype(jnp.float32), 0.0))
+        stacked = jnp.concatenate(
+            [
+                jnp.concatenate([basis[0], -basis[1]], 1),
+                jnp.concatenate([basis[1], basis[0]], 1),
+            ],
+            0,
+        ).astype(jnp.bfloat16)
+        here = slice(2 * slot * qpad, 2 * (slot + 1) * qpad)
+        applied.append(
+            lax.dot_general(green_high[:, here], stacked, NT, preferred_element_type=jnp.float32)
+            + lax.dot_general(green_low[:, here], stacked, NT, preferred_element_type=jnp.float32)
+        )
+        source = jnp.clip(row + slot - reach, 0, n_row - 1)
+        sources.append(both(jnp.concatenate([excite_all[half, source] for half in range(2)], 0)))
+    high, low = split_two(jnp.concatenate(applied, 1))
+    sources = jnp.concatenate(sources, 0)
+    inner = jnp.dot(high, sources, preferred_element_type=jnp.float32) + jnp.dot(
+        low, sources, preferred_element_type=jnp.float32
+    )
+    inner = inner * (1.0 / FOUR_PI)
+    loads[4].wait()
     tests = jnp.concatenate(
         [tweight_ref[0, :, pl.ds(begin, blk)], tweight_ref[1, :, pl.ds(begin, blk)]], 0
     )
@@ -337,7 +413,11 @@
         for copy in far_copies(d):
             copy.wait_send()
 
-    for index, buffer in enumerate((geom_all, weight_all, excite_all)):
+    @pl.loop(0, band)
+    def _(slot):
+        weight_to_pair(slot, col).wait_send()
+
+    for index, buffer in enumerate((geom_all, excite_all)):
         to_pair(index, buffer).wait_send()
 
 
@@ -360,27 +440,37 @@
     excite_rows = excite.T
     weight_rows = src_weights.transpose(0, 2, 1)
     vmem = pl.BlockSpec(memory_space=pltpu.VMEM)
-    smem = pl.BlockSpec(memory_space=pltpu.SMEM)
     hbm = pl.BlockSpec(memory_space=pl.ANY)
     dma = pltpu.SemaphoreType.DMA
     return pl.pallas_call(
         kernel,
         out_shape=jax.ShapeDtypeStruct((blk, excite.shape[0]), jnp.float32),
-        in_specs=[smem, smem, vmem, vmem, vmem, hbm, hbm, hbm, hbm],
+        in_specs=[hbm] * 9,
         out_specs=vmem,
         scratch_shapes=[
             pltpu.VMEM((band,) + src_nodes.shape, jnp.float32),
             pltpu.VMEM((2, band) + weight_rows.shape, jnp.bfloat16),
             pltpu.VMEM((2, n_row) + src_geom.shape, jnp.float32),
             pltpu.VMEM((2, n_row) + excite_rows.shape, jnp.bfloat16),
-            pltpu.VMEM((band, 2, qn, 2 * qpad), jnp.bfloat16),
+            pltpu.VMEM((qn, band * 2 * qpad), jnp.bfloat16),
+            pltpu.VMEM((qn, band * 2 * qpad), jnp.bfloat16),
+            pltpu.SMEM(wavenumber.shape, jnp.float32),
+            pltpu.SMEM(near_order.shape, jnp.int32),
+            pltpu.VMEM(tgt_geom.shape, jnp.float32),
+            pltpu.VMEM(tgt_nodes.shape, jnp.float32),
+            pltpu.VMEM(tgt_weights.shape, jnp.bfloat16),
+            pltpu.VMEM(src_nodes.shape, jnp.float32),
+            dma((6,)),
             dma((band,)),
             dma((band,)),
             dma((n_row,)),
             dma((n_row,)),
             dma((4,)),
-            dma((3,)),
-            dma((3,)),
+            dma((band,)),
+            dma((band,)),
+            dma((band,)),
+            dma((2,)),
+            dma((2,)),
         ],
         compiler_params=pltpu.CompilerParams(collective_id=0, has_side_effects=True),
         name="slab",

time: 23.2 us -> 20 us (0.86)
  Pallas kernels: 20.9 us -> 17.5 us
    pallas_call x1, Pallas kernels: 20.9 us -> 17.5 us  [on_device(): pl.pallas_call(kernel, out_shape=jax.ShapeDtypeStruct((blk, excite.shape[...]
where the time goes in v1:
time: 20 us; the launch traced here: 19.6 us
  Pallas kernels  17.5 us (88%)
  local copies, waits for them, and re-layouts  1.47 us (7%)
  between operations  0.66 us (3%)
    pallas_call x1, Pallas kernels, on_device(): pl.pallas_call(kernel, out_shape=jax.ShapeDtypeStruct((blk, excite.shape[...  17.5 us
    unnamed x1, local copies, waits for them, and re-layouts  1.47 us

profile of v1, /device:TPU:1, one launch (start us, length us, event | category | flops | bytes accessed | tf_op | source)
XLA Modules:
  0.0 19.6 jit_solution(326420298280583003)
XLA Ops:
  0.7 17.5 %slab.1 = f32[128,128]{1,0:T(8,128)} custom-call(f32[1]{0:T(128)S(6)} %copy.11.wave_hbm, s32[2,9]{1,0:T(2,128)} %order_hbm.1, f32[6,256]{1,0:T(8,128)} %tgt_hbm.1, f32[3,384]{1,0:T(4,128)} %tnode_hbm.1, bf16[2,192,256]{2,1,0:T(8,128)(2,1)} %tweight_hbm.1, f32[4,16]{1,0:T(4,128)} %geom_hbm.1, bf16[16,128]{1,0:T(8,128)(2,1)} %bitcast.3, f32[3,192]{1,0:T(4,128)} %snode_hbm.1, ...), custom_call_target="tpu_custom_call" | custom-call | tf_op jit(solution)/shard_map/slab/pallas_call | solution.py:445
  18.2 1.5 %copy.12 = f32[128,128]{1,0:T(8,128)} copy(f32[128,128]{1,0:T(8,128)} %slab.1) | data formatting | bytes 131072
